TPU v7x, 32 devices: a whole 2x2x4 slice. The times are simulated.
32 devices in a mesh: cfg: 2 (over y), src: 4 (over z), col: 2 (over x), half: 2 (over core).
Axes of the slice: x: 2, y: 2, z: 4, core: 2. Of those that a mesh axis runs over, the one named last changes fastest.
Arguments:
- perambulator: bfloat16 [8, 4, 2, 512, 512], P(('cfg', 'src'), None, None, ('col', 'half')), parts along dimension 0, may hold values from -0.25 to 0.25
- elemental: bfloat16 [1, 8, 2, 128, 128], P(None, ('cfg', 'src')), parts along dimension 1, may hold values from -0.5 to 0.5
- source_order: int32 [8], P('cfg'), parts along dimension 0, may hold values from 0 to 3, as said below
- column_order: int32 [8, 128], P(('cfg', 'src')), parts along dimension 0, may hold values from 0 to 127, each once within a row
Outputs:
- meson_matrix: float32 [8, 2, 1, 1, 4], P(('cfg', 'src')), parts along dimension 0
There are 2 independent parts, one for each index of `cfg`. A program takes and returns all parts, laid end to end along the dimension named above; each array names one. Nothing has to cross between parts.
Inputs may be any that keep to these rules, and one draw needn't show every extreme that they name: `source_order`: each of 0 to 3 appears once. `column_order`: each row holds each of 0 to 127 once.
All inputs are finite; a program needn't handle non-finite values.
Results may differ from a plain program's by a relative error of at most 0.0042.
Values may be sent and summed in bfloat16 or wider, within the bound.
A program may use at most 128 MiB of HBM per device.

v0:
```python
import jax
import jax.numpy as jnp
from jax import lax
from jax.sharding import PartitionSpec as P

spin_sign = (1.0, 1.0, -1.0, -1.0)


def complex_rows(coefficients):
    real_part = coefficients[..., 0, :, :]
    imag_part = coefficients[..., 1, :, :]
    upper_rows = jnp.stack([real_part, -imag_part], axis=-3)
    lower_rows = jnp.stack([imag_part, real_part], axis=-3)
    return jnp.stack([upper_rows, lower_rows], axis=-4)


def on_device(perambulator, elemental, source_order, column_order):
    operators, own_slots, _, eigen_count, _ = elemental.shape
    slot_count = perambulator.shape[1]
    block_cols = perambulator.shape[3]
    components = perambulator.shape[4]
    spin_count = components // eigen_count
    sign_vector = jnp.repeat(jnp.array(spin_sign, jnp.bfloat16), eigen_count)
    half_count = lax.axis_size("half")
    block_index = lax.axis_index("col") * half_count + lax.axis_index("half")
    reordered = jax.vmap(
        lambda matrices, ordering: matrices[:, :, ordering, :], in_axes=(1, 0), out_axes=1
    )(elemental, column_order)
    sorted_tiles = jnp.take(perambulator, source_order, axis=1) * sign_vector
    col_count = lax.axis_size("col")
    src_count = lax.axis_size("src")
    col_width = components // col_count
    first_row = block_index * block_cols
    spin_index = first_row // eigen_count
    offset = first_row % eigen_count
    own_rows = lax.dynamic_slice_in_dim(reordered, offset, block_cols, 3)
    received = lax.all_gather(reordered, "src", axis=1, tiled=True)
    piece_count = received.shape[1]
    coef_block = complex_rows(received)
    tile_view = sorted_tiles
    tile_view = tile_view.reshape(own_slots, piece_count, 2, block_cols, spin_count, eigen_count)
    product = jnp.einsum(
        "oqxymr,uqyjsr->ouqxsmj", coef_block, tile_view, preferred_element_type=jnp.float32
    )
    forward = product.reshape(operators, own_slots, piece_count, 2, components, block_cols).astype(
        jnp.bfloat16
    )
    outgoing = sorted_tiles.reshape(own_slots, slot_count, 2, block_cols, col_count, col_width)
    outgoing = jnp.transpose(outgoing, (0, 1, 4, 2, 3, 5)).reshape(
        own_slots, slot_count * col_count, 2, block_cols, col_width
    )
    arrived = lax.all_to_all(outgoing, ("src", "col"), split_axis=1, concat_axis=0, tiled=True)
    paired = lax.all_gather(arrived, "half", axis=3, tiled=True)
    paired = paired.reshape(
        src_count, col_count, own_slots, own_slots, 2, half_count * block_cols, col_width
    )
    spin_rows = lax.dynamic_slice_in_dim(
        paired, spin_index * eigen_count - lax.axis_index("col") * col_width, eigen_count, 6
    )
    product = jnp.einsum(
        "opxymr,ncvpykr->opnvxmck",
        complex_rows(own_rows),
        spin_rows,
        preferred_element_type=jnp.float32,
    )
    backward = product.astype(jnp.bfloat16).reshape(
        operators, own_slots, slot_count, 2, block_cols, components
    )
    pair_sums = jnp.einsum(
        "apqxij,bpqyji->pqabxy", forward, backward, preferred_element_type=jnp.float32
    )
    real_part = pair_sums[..., 0, 0] - pair_sums[..., 1, 1]
    imag_part = pair_sums[..., 0, 1] + pair_sums[..., 1, 0]
    partial_value = jnp.transpose(jnp.stack([real_part, imag_part], 0), (1, 0, 3, 4, 2))
    return lax.psum(partial_value, ("col", "half"))


def solution(mesh):
    return jax.shard_map(
        on_device,
        mesh=mesh,
        in_specs=(
            P(("cfg", "src"), None, None, ("col", "half"), None),
            P(None, ("cfg", "src"), None, None, None),
            P("cfg"),
            P(("cfg", "src"), None),
        ),
        out_specs=P(("cfg", "src"), None, None, None, None),
        check_vma=False,
    )
```

profile of v0, /device:TPU:0, one launch (start us, length us, event | category | flops | bytes accessed | tf_op | source)
XLA Modules:
  0.0 77.4 jit_solution(9819729270097999021)
XLA Ops:
  6.5 0.0 copy-start
  6.5 0.0 all-gather.4.cloned.1.call-start
  6.5 0.7 compare_and_fusion
  7.3 0.7 compare_select_fusion.1
  8.0 0.7 broadcast_bitcast_fusion
  8.7 0.0 copy-done
  8.7 0.6 gather_fusion
  9.3 0.2 fusion.7
  9.5 0.1 fusion.25
  9.6 0.1 pad_maximum_fusion
  9.7 0.0 copy-start.1
  9.7 0.0 copy-start.2
  9.7 33.1 %all_to_all.12 = bf16[1,8,2,128,256]{4,3,2,0,1:T(8,128)(2,1)} all-to-all(bf16[1,8,2,128,256]{4,3,2,0,1:T(8,128)(2,1)S(1)} %bitcast.104), channel_id=1, replica_groups=mesh['cfg'=2,'src'=4,'col'=2,'half'=2] {'src','col'}, dimensions={1} | all-to-all | bytes 2097152 | tf_op jit(solution)/shard_map/all_to_all | solution.py:52
  42.8 0.0 copy-start.3
  42.8 0.0 all-gather.4.cloned.1.call-update
  42.8 0.0 copy-done.1
  42.9 0.1 copy.49
  42.9 0.0 copy-done.2
  43.0 0.8 gather_fusion.1
  43.8 14.3 %all-gather.1 = bf16[8,128,128]{2,1,0:T(8,128)(2,1)S(1)} all-gather(bf16[2,128,128]{2,1,0:T(8,128)(2,1)S(1)} %bitcast.108), channel_id=3, replica_groups=mesh['cfg'=2,'src'=4,'col'=2,'half'=2] {'src'}, dimensions={0}, use_global_device_ids=true | all-gather | bytes 327680 | tf_op jit(solution)/shard_map/all_gather | solution.py:37
  58.2 0.0 copy-done.3
  58.2 0.6 fusion.1
  58.7 0.1 copy.25
  58.9 0.0 all-gather.4.cloned.1.call-done
  58.9 1.7 %fusion = bf16[1,1,4,1,2,128,2,256]{5,7,4,6,2,0,3,1:T(8,128)(2,1)S(1)} fusion(bf16[4,2,1,1,2,256,256]{6,5,4,1,0,3,2:T(8,128)(2,1)} %bitcast.110, s32[]{:T(128)S(6)} %select_n.40, bf16[1,1,1,2,128,128]{5,4,3,2,1,0:T(8,128)(2,1)S(1)} %get-tuple-element.18, bf16[1,1,1,2,128,128]{5,4,3,2,1,0:T(8,128)(2,1)S(1)} %get-tuple-element.17), kind=kOutput, calls=%fused_computation.4 | convolution fusion | flops 269221888 | bytes 2228228 | tf_op jit(solution)/shard_map/opxymr,ncvpykr->opnvxmck/dot_general | solution.py:60
  60.6 0.1 copy.22
  60.7 3.5 %convolution_bitcast_fusion = f32[4,2,2]{2,1,0:T(2,128)S(1)} fusion(bf16[4,2,512,128]{3,2,1,0:T(8,128)(2,1)S(1)} %bitcast.106, bf16[4,2,128,512]{2,3,1,0:T(8,128)(2,1)S(1)} %bitcast.107), kind=kOutput, calls=%fused_computation.6 | convolution fusion | flops 2097152 | bytes 2097216 | tf_op jit(solution)/shard_map/apqxij,bpqyji->pqabxy/dot_general | solution.py:69
  64.2 0.1 copy.28
  64.3 6.2 %psum.7 = f32[1,2,1,1,4]{4,1,3,2,0:T(2,128)} all-reduce(f32[1,2,1,1,4]{4,1,3,2,0:T(2,128)S(1)} %bitcast.113), channel_id=1, replica_groups=mesh['cfg'=2,'src'=4,'col'=2,'half'=2] {'col','half'}, use_global_device_ids=true, to_apply=%region_0.1 | all-reduce | flops 8 | bytes 64 | tf_op jit(solution)/shard_map/psum | solution.py:75
  (11 shorter events, 0.2 us)
Async XLA Ops:
  6.5 2.1 %copy-start = (bf16[1,4,2,128,512]{4,3,2,1,0:T(8,128)(2,1)S(1)}, bf16[1,4,2,128,512]{4,3,2,1,0:T(8,128)(2,1)}, u32[]{:S(2)}) copy-start(bf16[1,4,2,128,512]{4,3,2,1,0:T(8,128)(2,1)} %param.5) | copy-start | bytes 3145732
  6.5 52.3 %all-gather.4.cloned.1.call-start = ((), (), s32[]{:S(2)}) async-start(), calls=%async_computation.1 | async-start | bytes 3145728 | tf_op jit(solution)/shard_map/all_gather | solution.py:53
  9.7 33.2 %copy-start.1 = (bf16[1,1,2,128,128]{4,3,2,1,0:T(8,128)(2,1)S(1)}, bf16[1,1,2,128,128]{4,3,2,1,0:T(8,128)(2,1)}, u32[]{:S(2)}) copy-start(bf16[1,1,2,128,128]{4,3,2,1,0:T(8,128)(2,1)} %param.6) | copy-start | bytes 196612
  9.7 33.2 %copy-start.2 = (s32[1,128]{1,0:T(1,128)S(1)}, s32[1,128]{1,0:T(1,128)}, u32[]{:S(2)}) copy-start(s32[1,128]{1,0:T(1,128)} %param.8) | copy-start | bytes 1540
  42.8 15.4 %copy-start.3 = (bf16[4]{0:T(256)(128)(2,1)S(1)}, bf16[4]{0:T(256)(128)(2,1)}, u32[]{:S(2)}) copy-start(bf16[4]{0:T(256)(128)(2,1)} %constant.52.clone) | copy-start | bytes 28
Sparse Core Ops, SparseCore 0:
  42.9 9.5 all-gather.3
where the time goes:
time: 77.6 us; the launch traced here: 77.4 us
  blocking collectives  53.6 us (69%)
  between operations  13.6 us (18%)
  matrix products  5.73 us (7%)
  local copies, waits for them, and re-layouts  2.57 us (3%)
  other arithmetic  1.81 us (2%)
    all_to_all x1, blocking collectives, on_device(): lax.all_to_all(outgoing, ('src', 'col'), split_axis=1, concat_axis=0, til...  33.1 us
    all_gather x1, blocking collectives, on_device(): received = lax.all_gather(reordered, 'src', axis=1, tiled=True)  14.3 us
    psum x1, blocking collectives, on_device(): return lax.psum(partial_value, ('col', 'half'))  6.22 us
    dot_general x1, matrix products, on_device(): jnp.einsum('apqxij,bpqyji->pqabxy', forward, backward, preferred_element_...  3.47 us
    dot_general x1, matrix products, on_device(): jnp.einsum('opxymr,ncvpykr->opnvxmck', complex_rows(own_rows), spin_rows,...  1.7 us
  transfers between devices with their start and end apart: 1, of which 0 were waited for; matrix products, arithmetic and copies ran while one was open for 2% of the time, Pallas kernels for 0%

commit v1 on v0

v1 whole, which is shorter than its diff:
```python
import functools

import jax
import jax.numpy as jnp
from jax import lax
from jax.experimental import pallas as pl
from jax.experimental.pallas import tpu as pltpu
from jax.sharding import PartitionSpec as P

spin_sign = (1.0, 1.0, -1.0, -1.0)
MESH = pl.DeviceIdType.MESH
NT = (((1,), (1,)), ((), ()))


def dot_nt(a, b):
    return lax.dot_general(a, b, NT, preferred_element_type=jnp.float32)


def sends(source, target):
    even = lax.rem(source + target, 2) == 0
    return jnp.logical_and(even, source < target) | jnp.logical_and(
        jnp.logical_not(even), source > target
    )


def kernel(
    sizes,
    tiles_hbm, elem_hbm, order_hbm, column_hbm,
    out_ref,
    tiles, elem, order, column,
    sorted_tiles, coef, mirror, result,
    load_sem, tile_send, tile_recv, coef_send, coef_recv, share_send, share_recv,
    result_send, result_recv,
):
    src_count, col_count, half_count = sizes
    blocks = col_count * half_count
    block_cols, components = tiles.shape[2], tiles.shape[3]
    eigen = elem.shape[-1]
    spins = components // eigen
    piece = eigen // blocks
    p = lax.axis_index("src")
    b = lax.axis_index("col") * half_count + lax.axis_index("half")

    def device(slot, block):
        return {
            "src": slot,
            "col": lax.div(block, half_count),
            "half": lax.rem(block, half_count),
        }

    def wait_bytes(ref, sem):
        pltpu.make_async_copy(ref, ref, sem).wait()

    barrier = pltpu.get_barrier_semaphore()
    count = src_count * blocks
    me = p * blocks + b

    @pl.loop(1, count)
    def _(step):
        other = lax.rem(me + step, count)
        pl.semaphore_signal(
            barrier,
            inc=1,
            device_id=device(lax.div(other, blocks), lax.rem(other, blocks)),
            device_id_type=MESH,
        )

    loads = [
        pltpu.make_async_copy(order_hbm, order, load_sem.at[0]),
        pltpu.make_async_copy(tiles_hbm.at[0], tiles, load_sem.at[1]),
        pltpu.make_async_copy(elem_hbm.at[0, 0], elem, load_sem.at[2]),
        pltpu.make_async_copy(column_hbm, column, load_sem.at[3]),
    ]
    for load in loads:
        load.start()

    loads[2].wait()
    loads[3].wait()
    pick = (
        lax.broadcasted_iota(jnp.int32, (eigen, eigen), 0) == column[...]
    ).astype(jnp.float32).T.astype(jnp.bfloat16)
    both = jnp.concatenate([elem[0], elem[1]], axis=1)
    rows = jnp.dot(pick, both, preferred_element_type=jnp.float32).astype(jnp.bfloat16)
    coef[p, 0] = rows[:, :eigen]
    coef[p, 1] = rows[:, eigen:]

    loads[0].wait()
    loads[1].wait()

    @pl.loop(0, src_count)
    def _(slot):
        sorted_tiles[slot] = tiles[order[slot]]

    my_spin = lax.div(b * block_cols, eigen)
    my_lanes = pl.ds(pl.multiple_of(my_spin * eigen, eigen), eigen)
    my_rows = pl.ds(pl.multiple_of(b * block_cols, block_cols), block_cols)
    mirror[p, :, my_rows, :] = sorted_tiles[p, :, :, my_lanes]

    pl.semaphore_wait(barrier, count - 1)

    def partner(step):
        distance = src_count - 1 - lax.div(step, 2)
        slot = jnp.where(lax.rem(step, 2) == 0, p + distance, p - distance)
        valid = jnp.logical_and(slot >= 0, slot < src_count)
        return jnp.clip(slot, 0, src_count - 1), valid

    my_piece = pl.ds(pl.multiple_of(b * piece, piece), piece)

    def send_tile(slot, block):
        lanes = pl.ds(pl.multiple_of(lax.div(block * block_cols, eigen) * eigen, eigen), eigen)
        pltpu.make_async_remote_copy(
            src_ref=sorted_tiles.at[slot, :, :, lanes],
            dst_ref=mirror.at[p, :, my_rows, :],
            send_sem=tile_send.at[slot],
            recv_sem=tile_recv.at[p],
            device_id=device(slot, block),
            device_id_type=MESH,
        ).start()

    steps = 2 * (src_count - 1)

    @pl.loop(0, steps)
    def _(step):
        slot, valid = partner(step)

        @pl.when(jnp.logical_and(valid, sends(p, slot)))
        def _():
            pltpu.make_async_remote_copy(
                src_ref=coef.at[p, :, my_piece, :],
                dst_ref=coef.at[p, :, my_piece, :],
                send_sem=coef_send.at[slot],
                recv_sem=coef_recv.at[p],
                device_id={"src": slot},
                device_id_type=MESH,
            ).start()

    @pl.loop(0, steps)
    def _(step):
        slot, valid = partner(step)

        @pl.when(jnp.logical_and(valid, sends(p, slot)))
        def _():
            @pl.loop(0, blocks)
            def _(k):
                send_tile(slot, lax.rem(b + k, blocks))

    @pl.loop(1, blocks)
    def _(k):
        send_tile(p, lax.rem(b + k, blocks))

    @pl.loop(0, steps)
    def _(step):
        slot, valid = partner(step)

        @pl.when(jnp.logical_and(valid, sends(slot, p)))
        def _():
            wait_bytes(coef.at[slot, :, pl.ds(0, piece), :], coef_recv.at[slot])

            @pl.loop(1, blocks)
            def _(k):
                pltpu.make_async_remote_copy(
                    src_ref=coef.at[slot, :, my_piece, :],
                    dst_ref=coef.at[slot, :, my_piece, :],
                    send_sem=share_send.at[slot],
                    recv_sem=share_recv.at[slot],
                    device_id=device(p, lax.rem(b + k, blocks)),
                    device_id_type=MESH,
                ).start()

    def fold(value):
        return jnp.sum(value.reshape(block_cols // 8, 8, eigen), axis=0)

    offset = pl.ds(pl.multiple_of(lax.rem(b * block_cols, eigen), block_cols), block_cols)
    own_sign = jnp.where(my_spin < 2, spin_sign[0], spin_sign[2]).astype(jnp.float32)

    def pair(slot):
        own_real, own_imag = coef[p, 0, offset, :], coef[p, 1, offset, :]
        left = jnp.concatenate(
            [
                jnp.concatenate([own_real, -own_imag], axis=1),
                jnp.concatenate([own_imag, own_real], axis=1),
            ],
            axis=0,
        )
        far_real, far_imag = coef[slot, 0], coef[slot, 1]
        right = jnp.concatenate(
            [
                jnp.concatenate([far_real, -far_imag], axis=1),
                jnp.concatenate([far_imag, far_real], axis=1),
            ],
            axis=0,
        )
        total_real = jnp.zeros((8, eigen), jnp.float32)
        total_imag = jnp.zeros((8, eigen), jnp.float32)
        for spin in range(spins):
            part = slice(spin * eigen, (spin + 1) * eigen)
            near = jnp.concatenate(
                [sorted_tiles[slot, 0, :, part], sorted_tiles[slot, 1, :, part]], axis=1
            )
            away = jnp.concatenate([mirror[slot, 0, part, :], mirror[slot, 1, part, :]], axis=1)
            forward = dot_nt(near, right).astype(jnp.bfloat16).astype(jnp.float32)
            backward = dot_nt(left, away).astype(jnp.bfloat16).astype(jnp.float32)
            fr, fi = forward[:, :eigen], forward[:, eigen:]
            br, bi = backward[:block_cols], backward[block_cols:]
            total_real += spin_sign[spin] * fold(fr * br - fi * bi)
            total_imag += spin_sign[spin] * fold(fr * bi + fi * br)
        result[slot, b, 0] = own_sign * total_real
        result[slot, b, 1] = own_sign * total_imag

    def send_result(slot, target, block, there):
        pltpu.make_async_remote_copy(
            src_ref=result.at[slot, b],
            dst_ref=result.at[there, b],
            send_sem=result_send.at[slot],
            recv_sem=result_recv.at[there],
            device_id=device(target, block),
            device_id_type=MESH,
        ).start()

    def share_in_slot(slot):
        @pl.loop(1, blocks)
        def _(k):
            send_result(slot, p, lax.rem(b + k, blocks), slot)

    wait_bytes(mirror.at[p, :, pl.ds(0, components - block_cols), :], tile_recv.at[p])
    pair(p)
    share_in_slot(p)

    @pl.loop(0, steps)
    def _(step):
        slot, valid = partner(step)

        @pl.when(jnp.logical_and(valid, sends(slot, p)))
        def _():
            wait_bytes(coef.at[slot, :, pl.ds(0, eigen - piece), :], share_recv.at[slot])
            wait_bytes(mirror.at[slot], tile_recv.at[slot])
            pair(slot)

            @pl.loop(0, blocks)
            def _(k):
                send_result(slot, slot, lax.rem(b + k, blocks), p)

            share_in_slot(slot)

    lane = lax.broadcasted_iota(jnp.int32, (1, src_count), 1)

    def gather(slot, rows):
        real_row, imag_row = rows
        here = jnp.logical_or(slot == p, sends(slot, p))

        @pl.when(here)
        def _():
            wait_bytes(result.at[slot, pl.ds(0, blocks - 1)], result_recv.at[slot])

        @pl.when(jnp.logical_not(here))
        def _():
            wait_bytes(result.at[slot], result_recv.at[slot])

        total = jnp.sum(result[slot], axis=0)
        real_row = jnp.where(lane == slot, jnp.sum(total[0], keepdims=True), real_row)
        imag_row = jnp.where(lane == slot, jnp.sum(total[1], keepdims=True), imag_row)
        return real_row, imag_row

    zero = jnp.zeros((1, src_count), jnp.float32)
    real_row, imag_row = lax.fori_loop(0, src_count, gather, (zero, zero))
    out_ref[0, 0, 0] = real_row
    out_ref[0, 1, 0] = imag_row

    wait_bytes(mirror.at[p, :, pl.ds(0, components - block_cols), :], tile_send.at[p])
    wait_bytes(result.at[p, pl.ds(0, blocks - 1)], result_send.at[p])

    @pl.loop(0, steps)
    def _(step):
        slot, valid = partner(step)

        @pl.when(jnp.logical_and(valid, sends(p, slot)))
        def _():
            wait_bytes(coef.at[slot, :, pl.ds(0, piece), :], coef_send.at[slot])
            wait_bytes(mirror.at[slot], tile_send.at[slot])

        @pl.when(jnp.logical_and(valid, sends(slot, p)))
        def _():
            wait_bytes(coef.at[slot, :, pl.ds(0, eigen - piece), :], share_send.at[slot])
            wait_bytes(result.at[slot], result_send.at[slot])
            wait_bytes(result.at[slot, pl.ds(0, blocks - 1)], result_send.at[slot])


def on_device(sizes, perambulator, elemental, source_order, column_order):
    operators = elemental.shape[0]
    eigen = elemental.shape[-1]
    _, slots, _, block_cols, components = perambulator.shape
    src_count, col_count, half_count = sizes
    blocks = col_count * half_count
    sem = pltpu.SemaphoreType.DMA
    return pl.pallas_call(
        functools.partial(kernel, sizes),
        out_shape=jax.ShapeDtypeStruct((1, 2, operators, operators, slots), jnp.float32),
        in_specs=[pl.BlockSpec(memory_space=pl.ANY)] * 4,
        out_specs=pl.BlockSpec(memory_space=pltpu.VMEM),
        scratch_shapes=[
            pltpu.VMEM((slots, 2, block_cols, components), jnp.bfloat16),
            pltpu.VMEM((2, eigen, eigen), jnp.bfloat16),
            pltpu.SMEM((slots,), jnp.int32),
            pltpu.VMEM((1, eigen), jnp.int32),
            pltpu.VMEM((slots, 2, block_cols, components), jnp.bfloat16),
            pltpu.VMEM((slots, 2, eigen, eigen), jnp.bfloat16),
            pltpu.VMEM((slots, 2, components, eigen), jnp.bfloat16),
            pltpu.VMEM((slots, blocks, 2, 8, eigen), jnp.float32),
            sem((4,)),
        ]
        + [sem((slots,))] * 8,
        compiler_params=pltpu.CompilerParams(collective_id=0, has_side_effects=True),
    )(perambulator, elemental, source_order, column_order)


def solution(mesh):
    sizes = (mesh.shape["src"], mesh.shape["col"], mesh.shape["half"])
    return jax.shard_map(
        functools.partial(on_device, sizes),
        mesh=mesh,
        in_specs=(
            P(("cfg", "src"), None, None, ("col", "half"), None),
            P(None, ("cfg", "src"), None, None, None),
            P("cfg"),
            P(("cfg", "src"), None),
        ),
        out_specs=P(("cfg", "src"), None, None, None, None),
        check_vma=False,
    )
```

time: 77.6 us -> 25.5 us (0.33)
  blocking collectives: 53.6 us -> 0 us
  Pallas kernels: 0 us -> 24.1 us
  between operations: 13.6 us -> 0.01 us
  matrix products: 5.73 us -> 0 us
  other arithmetic: 1.81 us -> 0 us
  local copies, waits for them, and re-layouts: 2.57 us -> 1.24 us
    all_to_all x1 -> x0, blocking collectives: 33.1 us -> none  [on_device(): lax.all_to_all(outgoing, ('src', 'col'), split_axis=1, concat_axis=0, til...]
    pallas_call x0 -> x1, Pallas kernels: none -> 24.1 us  [on_device(): pl.pallas_call(functools.partial(kernel, sizes), out_shape=jax.ShapeDtype...]
    all_gather x1 -> x0, blocking collectives: 14.3 us -> none  [on_device(): received = lax.all_gather(reordered, 'src', axis=1, tiled=True)]
    psum x1 -> x0, blocking collectives: 6.22 us -> none  [on_device(): return lax.psum(partial_value, ('col', 'half'))]
    dot_general x3 -> x0, matrix products: 5.73 us -> none  [the longest x1 3.47 us: on_device(): jnp.einsum('apqxij,bpqyji->pqabxy', forward, backward, preferred_element_...]
    gather x4 -> x0, local copies, waits for them, and re-layouts: 1.38 us -> none  [the longest x3 0.77 us: on_device(): matrices[:, :, ordering, :]]
    unnamed x9 -> x1, local copies, waits for them, and re-layouts: 0.09 us -> 1.24 us
  transfers between devices with their start and end apart: 1 -> 0, of which waited for: 0 -> 0; matrix products, arithmetic and copies ran while one was open for 2% -> 0% of each run, Pallas kernels for 0% -> 0%
where the time goes in v1:
time: 25.5 us; the launch traced here: 25.4 us
  Pallas kernels  24.1 us (95%)
  local copies, waits for them, and re-layouts  1.24 us (5%)
    pallas_call x1, Pallas kernels, on_device(): pl.pallas_call(functools.partial(kernel, sizes), out_shape=jax.ShapeDtype...  24.1 us
    unnamed x1, local copies, waits for them, and re-layouts  1.24 us

profile of v1, /device:TPU:0, one launch (start us, length us, event | category | flops | bytes accessed | tf_op | source)
XLA Modules:
  0.0 25.4 jit_solution(11837882988034107740)
XLA Ops:
  0.0 24.1 %shard_map.46 = f32[1,2,1,1,4]{4,3,2,1,0:T(1,128)} custom-call(bf16[1,4,2,128,512]{4,3,2,1,0:T(8,128)(2,1)} %tiles_hbm.1, bf16[1,1,2,128,128]{4,3,2,1,0:T(8,128)(2,1)} %elem_hbm.1, s32[4]{0:T(128)} %order_hbm.1, s32[1,128]{1,0:T(1,128)} %column_hbm.1), custom_call_target="tpu_custom_call" | custom-call | tf_op jit(solution)/shard_map/pallas_call | solution.py:295
  24.1 1.2 %copy.6 = f32[1,2,1,1,4]{4,3,2,1,0:T(1,128)} copy(f32[1,2,1,1,4]{4,3,2,1,0:T(1,128)} %shard_map.46) | data formatting | bytes 64

commit v2 on v1

--- a/solution.py
+++ b/solution.py
@@ -99,7 +99,7 @@
     pl.semaphore_wait(barrier, count - 1)
 
     def partner(step):
-        distance = src_count - 1 - lax.div(step, 2)
+        distance = 1 + lax.div(step, 2)
         slot = jnp.where(lax.rem(step, 2) == 0, p + distance, p - distance)
         valid = jnp.logical_and(slot >= 0, slot < src_count)
         return jnp.clip(slot, 0, src_count - 1), valid
@@ -294,7 +294,7 @@
     sem = pltpu.SemaphoreType.DMA
     return pl.pallas_call(
         functools.partial(kernel, sizes),
-        out_shape=jax.ShapeDtypeStruct((1, 2, operators, operators, slots), jnp.float32),
+        out_shape=pltpu.VMEM((1, 2, operators, operators, slots), jnp.float32),
         in_specs=[pl.BlockSpec(memory_space=pl.ANY)] * 4,
         out_specs=pl.BlockSpec(memory_space=pltpu.VMEM),
         scratch_shapes=[

time: 25.5 us -> 23.8 us (0.933)
  Pallas kernels: 24.1 us -> 23.1 us
  local copies, waits for them, and re-layouts: 1.24 us -> 0.56 us
    pallas_call x1, Pallas kernels: 24.1 us -> 23.1 us  [on_device(): pl.pallas_call(functools.partial(kernel, sizes), out_shape=pltpu.VMEM((1,...]
    unnamed x1, local copies, waits for them, and re-layouts: 1.24 us -> 0.56 us
where the time goes in v2:
time: 23.8 us; the launch traced here: 23.6 us
  Pallas kernels  23.1 us (97%)
  local copies, waits for them, and re-layouts  0.56 us (2%)
    pallas_call x1, Pallas kernels, on_device(): pl.pallas_call(functools.partial(kernel, sizes), out_shape=pltpu.VMEM((1,...  23.1 us
    unnamed x1, local copies, waits for them, and re-layouts  0.56 us

profile of v2, /device:TPU:0, one launch (start us, length us, event | category | flops | bytes accessed | tf_op | source)
XLA Modules:
  0.0 23.6 jit_solution(2210261698581623237)
XLA Ops:
  0.0 23.1 %shard_map.46 = f32[1,2,1,1,4]{4,3,2,1,0:T(1,128)S(1)} custom-call(bf16[1,4,2,128,512]{4,3,2,1,0:T(8,128)(2,1)} %tiles_hbm.1, bf16[1,1,2,128,128]{4,3,2,1,0:T(8,128)(2,1)} %elem_hbm.1, s32[4]{0:T(128)} %order_hbm.1, s32[1,128]{1,0:T(1,128)} %column_hbm.1), custom_call_target="tpu_custom_call" | custom-call | tf_op jit(solution)/shard_map/pallas_call | solution.py:295
  23.1 0.6 %copy.6 = f32[1,2,1,1,4]{4,3,2,1,0:T(1,128)} copy(f32[1,2,1,1,4]{4,3,2,1,0:T(1,128)S(1)} %shard_map.46) | data formatting | bytes 64

commit v3 on v2

--- a/solution.py
+++ b/solution.py
@@ -242,30 +242,6 @@
 
             share_in_slot(slot)
 
-    lane = lax.broadcasted_iota(jnp.int32, (1, src_count), 1)
-
-    def gather(slot, rows):
-        real_row, imag_row = rows
-        here = jnp.logical_or(slot == p, sends(slot, p))
-
-        @pl.when(here)
-        def _():
-            wait_bytes(result.at[slot, pl.ds(0, blocks - 1)], result_recv.at[slot])
-
-        @pl.when(jnp.logical_not(here))
-        def _():
-            wait_bytes(result.at[slot], result_recv.at[slot])
-
-        total = jnp.sum(result[slot], axis=0)
-        real_row = jnp.where(lane == slot, jnp.sum(total[0], keepdims=True), real_row)
-        imag_row = jnp.where(lane == slot, jnp.sum(total[1], keepdims=True), imag_row)
-        return real_row, imag_row
-
-    zero = jnp.zeros((1, src_count), jnp.float32)
-    real_row, imag_row = lax.fori_loop(0, src_count, gather, (zero, zero))
-    out_ref[0, 0, 0] = real_row
-    out_ref[0, 1, 0] = imag_row
-
     wait_bytes(mirror.at[p, :, pl.ds(0, components - block_cols), :], tile_send.at[p])
     wait_bytes(result.at[p, pl.ds(0, blocks - 1)], result_send.at[p])
 
@@ -283,6 +259,27 @@
             wait_bytes(coef.at[slot, :, pl.ds(0, eigen - piece), :], share_send.at[slot])
             wait_bytes(result.at[slot], result_send.at[slot])
             wait_bytes(result.at[slot, pl.ds(0, blocks - 1)], result_send.at[slot])
+
+    @pl.loop(0, src_count)
+    def _(slot):
+        here = jnp.logical_or(slot == p, sends(slot, p))
+
+        @pl.when(here)
+        def _():
+            wait_bytes(result.at[slot, pl.ds(0, blocks - 1)], result_recv.at[slot])
+
+        @pl.when(jnp.logical_not(here))
+        def _():
+            wait_bytes(result.at[slot], result_recv.at[slot])
+
+    lane = lax.broadcasted_iota(jnp.int32, (1, src_count), 1)
+    rows = [jnp.zeros((1, src_count), jnp.float32)] * 2
+    for slot in range(src_count):
+        total = jnp.sum(result[slot], axis=0)
+        for part in (0, 1):
+            rows[part] = jnp.where(lane == slot, jnp.sum(total[part], keepdims=True), rows[part])
+    out_ref[0, 0, 0] = rows[0]
+    out_ref[0, 1, 0] = rows[1]
 
 
 def on_device(sizes, perambulator, elemental, source_order, column_order):

time: 23.8 us -> 23.6 us (level)
  no operation moved by 1% of the time
where the time goes in v3:
time: 23.6 us; the launch traced here: 23.5 us
  Pallas kernels  22.9 us (97%)
  local copies, waits for them, and re-layouts  0.56 us (2%)
    pallas_call x1, Pallas kernels, on_device(): pl.pallas_call(functools.partial(kernel, sizes), out_shape=pltpu.VMEM((1,...  22.9 us
    unnamed x1, local copies, waits for them, and re-layouts  0.56 us

profile of v3, /device:TPU:0, one launch (start us, length us, event | category | flops | bytes accessed | tf_op | source)
XLA Modules:
  0.0 23.5 jit_solution(7003336110123276945)
XLA Ops:
  0.0 22.9 %shard_map.46 = f32[1,2,1,1,4]{4,3,2,1,0:T(1,128)S(1)} custom-call(bf16[1,4,2,128,512]{4,3,2,1,0:T(8,128)(2,1)} %tiles_hbm.1, bf16[1,1,2,128,128]{4,3,2,1,0:T(8,128)(2,1)} %elem_hbm.1, s32[4]{0:T(128)} %order_hbm.1, s32[1,128]{1,0:T(1,128)} %column_hbm.1), custom_call_target="tpu_custom_call" | custom-call | tf_op jit(solution)/shard_map/pallas_call | solution.py:292
  22.9 0.6 %copy.6 = f32[1,2,1,1,4]{4,3,2,1,0:T(1,128)} copy(f32[1,2,1,1,4]{4,3,2,1,0:T(1,128)S(1)} %shard_map.46) | data formatting | bytes 64

commit v4 on v3

--- a/solution.py
+++ b/solution.py
@@ -55,7 +55,7 @@
     count = src_count * blocks
     me = p * blocks + b
 
-    @pl.loop(1, count)
+    @pl.loop(1, count, unroll=count <= 16)
     def _(step):
         other = lax.rem(me + step, count)
         pl.semaphore_signal(

time: 23.6 us -> 23.6 us (level)
  no operation moved by 1% of the time
where the time goes in v4:
time: 23.6 us; the launch traced here: 23.4 us
  Pallas kernels  22.9 us (97%)
  local copies, waits for them, and re-layouts  0.56 us (2%)
    pallas_call x1, Pallas kernels, on_device(): pl.pallas_call(functools.partial(kernel, sizes), out_shape=pltpu.VMEM((1,...  22.9 us
    unnamed x1, local copies, waits for them, and re-layouts  0.56 us

profile of v4, /device:TPU:0, one launch (start us, length us, event | category | flops | bytes accessed | tf_op | source)
XLA Modules:
  0.0 23.4 jit_solution(10208025240795799431)
XLA Ops:
  0.0 22.9 %shard_map.46 = f32[1,2,1,1,4]{4,3,2,1,0:T(1,128)S(1)} custom-call(bf16[1,4,2,128,512]{4,3,2,1,0:T(8,128)(2,1)} %tiles_hbm.1, bf16[1,1,2,128,128]{4,3,2,1,0:T(8,128)(2,1)} %elem_hbm.1, s32[4]{0:T(128)} %order_hbm.1, s32[1,128]{1,0:T(1,128)} %column_hbm.1), custom_call_target="tpu_custom_call" | custom-call | tf_op jit(solution)/shard_map/pallas_call | solution.py:292
  22.9 0.6 %copy.6 = f32[1,2,1,1,4]{4,3,2,1,0:T(1,128)} copy(f32[1,2,1,1,4]{4,3,2,1,0:T(1,128)S(1)} %shard_map.46) | data formatting | bytes 64
